TPU v7x, 256 devices: a whole 4x4x8 slice. The times are simulated.
256 devices in a mesh: seq: 32 (over x, z), mp: 8 (over y, core).
Axes of the slice: x: 4, y: 4, z: 8, core: 2. Of those that a mesh axis runs over, the one named last changes fastest.
Arguments:
- hidden_in: bfloat16 [64, 2048], P('mp'), may hold values from -24 to 24
- query_weight: bfloat16 [2048, 3072], P(None, 'seq'), may hold values from -0.25 to 0.25
- key_absorb: bfloat16 [16, 128, 512], replicated, may hold values from -0.5 to 0.5
- value_up: bfloat16 [16, 512, 128], replicated, may hold values from -0.25 to 0.25
- out_weight: bfloat16 [2048, 2048], P(None, 'seq'), may hold values from -0.5 to 0.5
- latent_cache: bfloat16 [64, 4096, 576], P('mp', 'seq'), may hold values from -41 to 41
- cache_lengths: int32 [64], P('mp'), may hold values from 128 to 4096, as said below
- keep_lists: int32 [64, 32, 64], P('mp', 'seq'), may hold values from 0 to 127, as said below
- drop_weights: int32 [64, 4096], P('mp', 'seq'), may hold values from 1 to 8
- pack_dest: int32 [64, 32], P('mp'), may hold values from -1 to 127, as said below
- final_gain: bfloat16 [2048], replicated, may hold values from 0.5 to 1.5
- head_weight: bfloat16 [2048, 102400], P(None, ('seq', 'mp')), may hold values from -0.125 to 0.125
- tenant_ranges: int32 [4, 2], replicated, may hold values from 0 to 102400, as said below
- tenant_ids: int32 [64], replicated, may hold values from 0 to 3
Outputs:
- packed_rows: bfloat16 [1024, 64, 576], P(('seq', 'mp'))
- packed_summary: bfloat16 [1024, 576], P(('seq', 'mp'))
- hidden_out: bfloat16 [64, 2048], P('mp', 'seq')
- state_norm: float32 [64], P('mp')
- top_logit: float32 [64], P('mp')
Inputs may be any that keep to these rules, and one draw needn't show every extreme that they name: `cache_lengths`: every length is a whole number of 128-position blocks, at least one block. Within each group of 8 requests (one index of mp) the lengths add up to 16384, and some request of the group has the full 4096. `keep_lists`: the 64 positions of a block are distinct and ascending. pack_dest[r, b] is -1 exactly when block b of request r is not live; otherwise it is owner * 4 + slot with an owner in 0 to 32 - 1 (an index of seq) and a slot in 0 to 3. Within one group of 8 requests the live blocks take every destination exactly once. Of the live blocks of one block index in one group, at most 1 go to any one owner, and those that share an owner take consecutive slots. Block index 0 is live for every request of a group, and some owner receives 1 of them. `tenant_ranges`: row t is tenant t's window [low, high) of vocabulary entries; each window holds at least 51200 entries.
All inputs are finite; a program needn't handle non-finite values.
Results may differ from a plain program's by a relative error of at most 0.0075.
Values may be sent and summed in bfloat16 or wider, within the bound.
No kernel may reach another device: no remote copies, remote signals or barrier semaphores. Data moves between devices by JAX's collectives and lax.ppermute only.
A program may use at most 128 MiB of HBM per device.

v0:
```python
import jax
import jax.numpy as jnp
from jax import lax
from jax.sharding import PartitionSpec as P

H = 16
NOPE = 128
ROPE = 64
LAT = 512
VH = 128
BLK = 128
KB = 64
TENANTS = 4
RQ = 8
NEGATIVE = -1e30
HIGHEST = lax.Precision.HIGHEST


def merged(x, axis, combine):
    everything = jax.tree.map(lambda part: lax.all_gather(part, axis), x)
    initial = jax.tree.map(lambda part: part[0], everything)

    def step(k, so_far):
        return combine(so_far, jax.tree.map(lambda part: part[k], everything))

    return lax.fori_loop(1, lax.axis_size(axis), step, initial)


def compact_blocks(block_rows, keep_onehot, weights_dropped):
    kept_rows = jnp.einsum(
        "nkt,ntc->nkc", keep_onehot, block_rows, preferred_element_type=jnp.float32
    ).astype(jnp.bfloat16)
    weight_mass = jnp.sum(weights_dropped.astype(jnp.float32), axis=1)
    summed = jnp.einsum(
        "nt,ntc->nc", weights_dropped, block_rows, preferred_element_type=jnp.float32
    )
    summary = (summed / weight_mass[:, None]).astype(jnp.bfloat16)
    return (kept_rows, summary)


def attend_blocks(query_lat, query_rope, kept_rows, summary, usable):
    score_scale = (NOPE + ROPE) ** (-0.5)
    row_scores = (
        jnp.einsum(
            "nhl,nkl->nhk", query_lat, kept_rows[:, :, :LAT], preferred_element_type=jnp.float32
        )
        + jnp.einsum(
            "nhr,nkr->nhk", query_rope, kept_rows[:, :, LAT:], preferred_element_type=jnp.float32
        )
    ) * score_scale
    summ_scores = (
        jnp.einsum("nhl,nl->nh", query_lat, summary[:, :LAT], preferred_element_type=jnp.float32)
        + jnp.einsum("nhr,nr->nh", query_rope, summary[:, LAT:], preferred_element_type=jnp.float32)
    ) * score_scale
    summ_scores = summ_scores + jnp.log(jnp.float32(BLK - KB))
    row_scores = jnp.where(usable[:, None, None], row_scores, NEGATIVE)
    summ_scores = jnp.where(usable[:, None], summ_scores, NEGATIVE)
    maxima = jnp.maximum(jnp.max(row_scores, axis=2), summ_scores)
    row_weights = jnp.where(usable[:, None, None], jnp.exp(row_scores - maxima[:, :, None]), 0.0)
    summ_weights = jnp.where(usable[:, None], jnp.exp(summ_scores - maxima), 0.0)
    totals = jnp.sum(row_weights, axis=2) + summ_weights
    weighted = jnp.einsum(
        "nhk,nkl->nhl", row_weights, kept_rows[:, :, :LAT].astype(jnp.float32), precision=HIGHEST
    )
    weighted = weighted + summ_weights[:, :, None] * summary[:, None, :LAT].astype(jnp.float32)
    return (maxima, totals, weighted)


def per_request(maxima, totals, weighted, owner_of):
    request_max = jnp.max(jnp.where(owner_of[:, :, None], maxima[None, :, :], NEGATIVE), axis=1)
    shifted = jnp.where(owner_of[:, :, None], maxima[None, :, :] - request_max[:, None, :], 0.0)
    factor = jnp.where(owner_of[:, :, None], jnp.exp(shifted), 0.0)
    request_total = jnp.einsum("rnh,nh->rh", factor, totals, precision=HIGHEST)
    request_sum = jnp.einsum("rnh,nhl->rhl", factor, weighted, precision=HIGHEST)
    return (request_max, request_total, request_sum)


def combine_partial(former, latter):
    former_max, former_total, former_sum = former
    latter_max, latter_total, latter_sum = latter
    joined = jnp.maximum(former_max, latter_max)
    former_factor = jnp.exp(former_max - joined)
    latter_factor = jnp.exp(latter_max - joined)
    return (
        joined,
        former_factor * former_total + latter_factor * latter_total,
        former_factor[:, :, None] * former_sum + latter_factor[:, :, None] * latter_sum,
    )


def body(
    hidden_in,
    query_weight,
    key_absorb,
    value_up,
    out_weight,
    latent_cache,
    cache_lengths,
    keep_lists,
    drop_weights,
    pack_dest,
    final_gain,
    head_weight,
    tenant_ranges,
    tenant_ids,
):
    seq_count = lax.axis_size("seq")
    mp_count = lax.axis_size("mp")
    seq_index = lax.axis_index("seq")
    mp_index = lax.axis_index("mp")
    capacity = max(1, RQ // seq_count)
    slot_count = RQ // 2
    row_width = LAT + ROPE
    query_part = jnp.dot(hidden_in, query_weight, preferred_element_type=jnp.float32).astype(
        jnp.bfloat16
    )
    query_full = lax.all_gather(query_part, "seq", axis=1, tiled=True).reshape(RQ, H, NOPE + ROPE)
    query_lat = jnp.einsum(
        "rhn,hnl->rhl", query_full[:, :, :NOPE], key_absorb, preferred_element_type=jnp.float32
    ).astype(jnp.bfloat16)
    query_rope = query_full[:, :, NOPE:]
    positions = jnp.arange(BLK, dtype=jnp.int32)
    keep_onehot = keep_lists[:, 0, :, None] == positions[None, None, :]
    kept_flag = jnp.sum(keep_onehot.astype(jnp.int32), axis=1)
    weights_dropped = (drop_weights * (1 - kept_flag)).astype(jnp.bfloat16)
    live_here = cache_lengths > seq_index * BLK
    dest_here = lax.dynamic_slice_in_dim(pack_dest, seq_index, 1, 1)[:, 0]
    send_slot = dest_here // slot_count * capacity + dest_here % slot_count % capacity
    slot_range = jnp.arange(seq_count * capacity, dtype=jnp.int32)
    send_onehot = ((send_slot[None, :] == slot_range[:, None]) & live_here[None, :]).astype(
        jnp.bfloat16
    )
    targets = seq_index * slot_count + jnp.arange(slot_count, dtype=jnp.int32)
    slot_match = (pack_dest[None, :, :] == targets[:, None, None]).astype(jnp.int32)
    block_range = jnp.arange(pack_dest.shape[1], dtype=jnp.int32)
    source_of = jnp.sum(slot_match * block_range[None, None, :], axis=(1, 2))
    request_of = jnp.sum(slot_match, axis=2)
    request_index = jnp.sum(request_of * jnp.arange(RQ, dtype=jnp.int32)[None, :], axis=1)
    pick_index = source_of * capacity + jnp.arange(slot_count, dtype=jnp.int32) % capacity
    owner_of = jnp.transpose(request_of) > 0
    local_rows, local_summary = compact_blocks(
        latent_cache, keep_onehot.astype(jnp.bfloat16), weights_dropped
    )
    send_rows = jnp.einsum(
        "jr,rkc->jkc", send_onehot, local_rows, preferred_element_type=jnp.float32
    )
    send_rows = send_rows.astype(jnp.bfloat16).reshape(seq_count, capacity, KB, row_width)
    send_summary = jnp.dot(send_onehot, local_summary, preferred_element_type=jnp.float32)
    send_summary = send_summary.astype(jnp.bfloat16).reshape(seq_count, capacity, row_width)
    recv_rows, recv_summary = (
        lax.all_to_all(send_rows, "seq", split_axis=0, concat_axis=0, tiled=True),
        lax.all_to_all(send_summary, "seq", split_axis=0, concat_axis=0, tiled=True),
    )
    packed_rows = jnp.take(
        recv_rows.reshape(seq_count * capacity, KB, row_width), pick_index, axis=0
    )
    packed_summary = jnp.take(
        recv_summary.reshape(seq_count * capacity, row_width), pick_index, axis=0
    )
    slot_query_lat = jnp.take(query_lat, request_index, axis=0)
    slot_query_rope = jnp.take(query_rope, request_index, axis=0)
    usable = jnp.ones((slot_count,), dtype=bool)
    maxima, totals, weighted = attend_blocks(
        slot_query_lat, slot_query_rope, packed_rows, packed_summary, usable
    )
    partial_value = per_request(maxima, totals, weighted, owner_of)
    request_max, request_total, request_sum = merged(partial_value, "seq", combine_partial)
    attended = (request_sum / request_total[:, :, None]).astype(jnp.bfloat16)
    values = jnp.einsum("rhl,hlv->rhv", attended, value_up, preferred_element_type=jnp.float32)
    values = values.astype(jnp.bfloat16).reshape(RQ, H * VH)
    col_width = out_weight.shape[1]
    residual = lax.dynamic_slice_in_dim(hidden_in, seq_index * col_width, col_width, 1)
    hidden_out = (
        residual.astype(jnp.float32)
        + jnp.dot(values, out_weight, preferred_element_type=jnp.float32)
    ).astype(jnp.bfloat16)
    gathered = lax.all_gather(hidden_out[None], ("seq", "mp"), axis=0, tiled=True)
    all_rows = gathered.reshape(seq_count, mp_count, RQ, col_width).transpose(1, 2, 0, 3)
    all_rows = all_rows.reshape(mp_count * RQ, seq_count * col_width)
    rows_f = all_rows.astype(jnp.float32)
    mean_sq = jnp.mean(rows_f * rows_f, axis=1)
    norms_all = jnp.sqrt(mean_sq)
    normed = (
        rows_f * lax.rsqrt(mean_sq + 1e-06)[:, None] * final_gain.astype(jnp.float32)[None, :]
    ).astype(jnp.bfloat16)
    logits = jnp.dot(normed, head_weight, preferred_element_type=jnp.float32)
    vocab_width = head_weight.shape[1]
    device_index = seq_index * mp_count + mp_index
    columns = device_index * vocab_width + jnp.arange(vocab_width, dtype=jnp.int32)
    tenant_onehot = (tenant_ids[:, None] == jnp.arange(TENANTS, dtype=jnp.int32)[None, :]).astype(
        jnp.int32
    )
    window_low = jnp.sum(tenant_onehot * tenant_ranges[None, :, 0], axis=1)
    window_high = jnp.sum(tenant_onehot * tenant_ranges[None, :, 1], axis=1)
    allowed = (columns[None, :] >= window_low[:, None]) & (columns[None, :] < window_high[:, None])
    local_best = jnp.max(jnp.where(allowed, logits, NEGATIVE), axis=1)
    best_all = lax.pmax(local_best, ("seq", "mp"))
    row_start = mp_index * RQ
    state_norm = lax.dynamic_slice_in_dim(norms_all, row_start, RQ, 0)
    top_logit = lax.dynamic_slice_in_dim(best_all, row_start, RQ, 0)
    return (packed_rows, packed_summary, hidden_out, state_norm, top_logit)


def solution(mesh):
    in_specs = (
        P("mp", None),
        P(None, "seq"),
        P(),
        P(),
        P(None, "seq"),
        P("mp", "seq", None),
        P("mp"),
        P("mp", "seq", None),
        P("mp", "seq"),
        P("mp", None),
        P(),
        P(None, ("seq", "mp")),
        P(),
        P(),
    )
    out_specs = (
        P(("seq", "mp"), None, None),
        P(("seq", "mp"), None),
        P("mp", "seq"),
        P("mp"),
        P("mp"),
    )
    return jax.shard_map(body, mesh=mesh, in_specs=in_specs, out_specs=out_specs, check_vma=False)
```

profile of v0, /device:TPU:1, one launch (start us, length us, event | category | flops | bytes accessed | tf_op | source)
XLA Modules:
  0.0 443.5 jit_solution(3956830009259574971)
XLA Ops:
  7.2 1.0 dynamic-slice_reduce_fusion
  10.5 1.7 fusion.37
  14.5 11.9 %all-to-all-start.1 = ((bf16[32,2,288]{2,1,0:T(2,128)(2,1)}), bf16[32,2,288]{2,1,0:T(2,128)(2,1)S(1)}, u32[]{:S(2)}, u32[]{:S(2)}) async-start(bf16[32,2,288]{2,1,0:T(2,128)(2,1)} %reshape.212), calls=%async_computation.1 | async-start | bytes 98304 | tf_op jit(solution)/shard_map/all_to_all | solution.py:152
  26.3 1.2 convolution_convert_fusion
  28.6 2.4 copy.83
  31.0 4.1 all-to-all-done.1
  35.1 5.3 %all-to-all-start = ((bf16[32,1,64,576]{3,2,1,0:T(8,128)(2,1)}), bf16[32,1,64,576]{3,2,1,0:T(8,128)(2,1)}, u32[]{:S(2)}, u32[]{:S(2)}) async-start(bf16[32,1,64,576]{3,2,1,0:T(8,128)(2,1)} %copy.83), calls=%async_computation | async-start | bytes 5242880 | tf_op jit(solution)/shard_map/all_to_all | solution.py:151
  40.8 88.3 %all-gather.4 = bf16[32,96,8]{1,2,0:T(8,128)(2,1)S(1)} all-gather(bf16[1,96,8]{1,2,0:T(8,128)(2,1)S(1)} %fusion.10), channel_id=1, replica_groups=mesh['seq'=32,'mp'=8] {'seq'}, dimensions={0}, use_global_device_ids=true | all-gather | bytes 50688 | tf_op jit(solution)/shard_map/all_gather | solution.py:117
  132.6 2.4 gather_fusion
  136.4 1.2 convolution_bitcast_fusion
  137.8 33.3 %all-gather = f32[256,16]{1,0:T(8,128)S(1)} all-gather(f32[8,16]{1,0:T(8,128)S(1)} %copy.89), channel_id=2, replica_groups=mesh['seq'=32,'mp'=8] {'seq'}, dimensions={0}, use_global_device_ids=true | all-gather | bytes 16896 | tf_op jit(solution)/shard_map/all_gather | solution.py:20
  171.4 33.9 %all-gather.1 = f32[256,16]{1,0:T(8,128)S(1)} all-gather(f32[8,16]{1,0:T(8,128)S(1)} %bitcast.111), channel_id=3, replica_groups=mesh['seq'=32,'mp'=8] {'seq'}, dimensions={0}, use_global_device_ids=true | all-gather | bytes 16896 | tf_op jit(solution)/shard_map/all_gather | solution.py:20
  205.4 41.6 %all-gather.7.cloned.1.call-done = f32[256,16,512]{2,0,1:T(8,128)} async-done(((f32[8,16,512]{2,0,1:T(8,128)}), f32[256,16,512]{2,0,1:T(8,128)}) %all-gather.7.cloned.1.call-update) | async-done | bytes 8388624 | tf_op jit(solution)/shard_map/all_gather | solution.py:20
  248.1 38.1 %while.19 = (s32[]{:T(128)}, f32[8,16]{1,0:T(8,128)S(1)}, f32[8,16]{1,0:T(8,128)S(1)}, f32[8,16,512]{2,1,0:T(8,128)S(1)}, f32[32,8,16]{2,1,0:T(8,128)S(1)}, /*in...) while((s32[]{:T(128)}, f32[8,16]{1,0:T(8,128)S(1)}, ...), condition=%wide.region_9.10_spmd, body=%wide.region_8.9_spmd.sunk | while | flops 197381 | bytes 1315991 | solution.py:26
  248.1 1.0 constant_dynamic-slice_fusion.2
  249.4 1.0 constant_dynamic-slice_fusion.2
  250.6 1.0 constant_dynamic-slice_fusion.2
  251.9 1.0 constant_dynamic-slice_fusion.2
  253.1 1.0 constant_dynamic-slice_fusion.2
  254.3 1.0 constant_dynamic-slice_fusion.2
  255.5 1.0 constant_dynamic-slice_fusion.2
  256.8 1.0 constant_dynamic-slice_fusion.2
  258.0 1.0 constant_dynamic-slice_fusion.2
  259.2 1.0 constant_dynamic-slice_fusion.2
  260.4 1.0 constant_dynamic-slice_fusion.2
  261.7 1.0 constant_dynamic-slice_fusion.2
  262.9 1.0 constant_dynamic-slice_fusion.2
  264.1 1.0 constant_dynamic-slice_fusion.2
  265.4 1.0 constant_dynamic-slice_fusion.2
  266.6 1.0 constant_dynamic-slice_fusion.2
  267.8 1.0 constant_dynamic-slice_fusion.2
  269.0 1.0 constant_dynamic-slice_fusion.2
  270.3 1.0 constant_dynamic-slice_fusion.2
  271.5 1.0 constant_dynamic-slice_fusion.2
  272.7 1.0 constant_dynamic-slice_fusion.2
  274.0 1.0 constant_dynamic-slice_fusion.2
  275.2 1.0 constant_dynamic-slice_fusion.2
  276.4 1.0 constant_dynamic-slice_fusion.2
  277.6 1.0 constant_dynamic-slice_fusion.2
  278.9 1.0 constant_dynamic-slice_fusion.2
  280.1 1.0 constant_dynamic-slice_fusion.2
  285.0 1.0 constant_dynamic-slice_fusion.2
  286.3 2.1 fusion.9
  288.4 67.2 %all-gather.3 = bf16[2048,64]{1,0:T(8,128)(2,1)S(1)} all-gather(bf16[8,64]{1,0:T(8,128)(2,1)S(1)} %fusion.9), channel_id=5, replica_groups=mesh['seq'=32,'mp'=8] {'seq','mp'}, dimensions={0}, use_global_device_ids=true | all-gather | bytes 263168 | tf_op jit(solution)/shard_map/all_gather | solution.py:177
  356.2 1.3 copy.135
  357.5 1.6 reshape.150
  359.2 2.2 fusion.5
  361.3 74.2 %pmax.7 = f32[64]{0:T(128)S(1)} all-reduce(f32[64]{0:T(128)S(1)} %fusion.5), channel_id=1, replica_groups=mesh['seq'=32,'mp'=8] {'seq','mp'}, use_global_device_ids=true, to_apply=%region_15.16 | all-reduce | flops 64 | bytes 512 | tf_op jit(solution)/shard_map/pmax | solution.py:197
  (158 shorter events, 23.9 us)
Async XLA Ops:
  7.2 122.2 %copy-start = (bf16[16,128,512]{2,1,0:T(8,128)(2,1)S(1)}, bf16[16,128,512]{2,1,0:T(8,128)(2,1)}, u32[]{:S(2)}) copy-start(bf16[16,128,512]{2,1,0:T(8,128)(2,1)} %param.18) | copy-start | bytes 6291460
  7.2 19.2 %copy-start.1 = (bf16[8,128,576]{1,2,0:T(8,128)(2,1)S(1)}, bf16[8,128,576]{1,2,0:T(8,128)(2,1)}, u32[]{:S(2)}) copy-start(bf16[8,128,576]{1,2,0:T(8,128)(2,1)} %param.21) | copy-start | bytes 3538948
  14.5 20.7 %all-to-all-start.1 = ((bf16[32,2,288]{2,1,0:T(2,128)(2,1)}), bf16[32,2,288]{2,1,0:T(2,128)(2,1)S(1)}, u32[]{:S(2)}, u32[]{:S(2)}) async-start(bf16[32,2,288]{2,1,0:T(2,128)(2,1)} %reshape.212), calls=%async_computation.1 | async-start | bytes 98304 | tf_op jit(solution)/shard_map/all_to_all | solution.py:152
  31.0 9.5 %copy-start.3 = (bf16[2048,96]{0,1:T(8,128)(2,1)S(1)}, bf16[2048,96]{0,1:T(8,128)(2,1)}, u32[]{:S(2)}) copy-start(bf16[2048,96]{0,1:T(8,128)(2,1)} %param.17) | copy-start | bytes 1179652
  31.0 9.6 %copy-start.5 = (bf16[8,2048]{1,0:T(8,128)(2,1)S(1)}, bf16[8,2048]{1,0:T(8,128)(2,1)}, u32[]{:S(2)}) copy-start(bf16[8,2048]{1,0:T(8,128)(2,1)} %param.16) | copy-start | bytes 98308
  35.1 97.5 %all-to-all-start = ((bf16[32,1,64,576]{3,2,1,0:T(8,128)(2,1)}), bf16[32,1,64,576]{3,2,1,0:T(8,128)(2,1)}, u32[]{:S(2)}, u32[]{:S(2)}) async-start(bf16[32,1,64,576]{3,2,1,0:T(8,128)(2,1)} %copy.83), calls=%async_computation | async-start | bytes 5242880 | tf_op jit(solution)/shard_map/all_to_all | solution.py:151
  40.5 89.3 %copy-start.7 = (s32[8,32]{1,0:T(8,128)S(1)}, s32[8,32]{1,0:T(8,128)}, u32[]{:S(2)}) copy-start(s32[8,32]{1,0:T(8,128)} %param.25) | copy-start | bytes 3076
  40.5 206.4 %all-gather.7.cloned.1.call-start = ((), (), s32[]{:S(2)}) async-start(), calls=%async_computation.2 | async-start | bytes 8650752 | tf_op jit(solution)/shard_map/all_gather | solution.py:20
  129.7 7.9 %copy-start.9 = (bf16[2048]{0:T(1024)(128)(2,1)S(1)}, bf16[2048]{0:T(1024)(128)(2,1)}, u32[]{:S(2)}) copy-start(bf16[2048]{0:T(1024)(128)(2,1)} %param.26) | copy-start | bytes 12292
  129.7 7.9 %copy-start.10 = (s32[4,2]{0,1:T(2,128)S(1)}, s32[4,2]{0,1:T(2,128)}, u32[]{:S(2)}) copy-start(s32[4,2]{0,1:T(2,128)} %param.28) | copy-start | bytes 100
  129.7 7.9 %copy-start.11 = (s32[64]{0:T(128)S(1)}, s32[64]{0:T(128)}, u32[]{:S(2)}) copy-start(s32[64]{0:T(128)} %param.29) | copy-start | bytes 772
  132.2 115.7 %copy-start.6 = (bf16[4,576]{1,0:T(4,128)(2,1)}, bf16[4,576]{1,0:T(4,128)(2,1)S(1)}, u32[]{:S(2)}) copy-start(bf16[4,576]{1,0:T(4,128)(2,1)S(1)} %broadcast_select_fusion.7) | copy-start | bytes 13828
  135.1 113.0 %copy-start.2 = (bf16[4,64,576]{2,1,0:T(8,128)(2,1)}, bf16[4,64,576]{2,1,0:T(8,128)(2,1)S(1)}, u32[]{:S(2)}) copy-start(bf16[4,64,576]{2,1,0:T(8,128)(2,1)S(1)} %broadcast_select_fusion) | copy-start | bytes 884740
  248.1 38.2 %copy-start.4 = (bf16[2048,64]{0,1:T(8,128)(2,1)S(1)}, bf16[2048,64]{0,1:T(8,128)(2,1)}, u32[]{:S(2)}) copy-start(bf16[2048,64]{0,1:T(8,128)(2,1)} %param.20) | copy-start | bytes 786436
  288.4 70.7 %copy-start.8 = (bf16[8,64]{1,0:T(8,128)(2,1)}, bf16[8,64]{1,0:T(8,128)(2,1)S(1)}, u32[]{:S(2)}) copy-start(bf16[8,64]{1,0:T(8,128)(2,1)S(1)} %fusion.9) | copy-start | bytes 3076
Sparse Core Ops, SparseCore 0:
  137.7 109.1 all-gather.6
where the time goes:
time: 445 us; the launch traced here: 444 us
  blocking collectives  297 us (67%)
  waiting for transfers between devices  45.7 us (10%)
  local copies, waits for them, and re-layouts  45.3 us (10%)
  starting transfers between devices  17.2 us (4%)
  between operations  14.5 us (3%)
  other arithmetic  11.5 us (3%)
  matrix products  11.5 us (3%)
    all_gather x1, blocking collectives, body(): lax.all_gather(query_part, 'seq', axis=1, tiled=True)  88.3 us
    pmax x1, blocking collectives, body(): best_all = lax.pmax(local_best, ('seq', 'mp'))  74.2 us
    all_gather x2, blocking collectives, merged(): everything = jax.tree.map(lambda part: lax.all_gather(part, axis), x)  67.2 us
    all_gather x1, blocking collectives, body(): lax.all_gather(hidden_out[None], ('seq', 'mp'), axis=0, tiled=True)  67.2 us
    all_gather x1, waiting for transfers between devices, merged(): everything = jax.tree.map(lambda part: lax.all_gather(part, axis), x)  41.6 us
    dynamic_slice x31, local copies, waits for them, and re-layouts, step(): return combine(so_far, jax.tree.map(lambda part: part[k], everything))  30.3 us
    all_to_all x1, starting transfers between devices, body(): lax.all_to_all(send_summary, 'seq', split_axis=0, concat_axis=0, tiled=True)  11.9 us
  transfers between devices with their start and end apart: 3, of which 2 were waited for; matrix products, arithmetic and copies ran while one was open for 2% of the time, Pallas kernels for 0%

commit v1 on v0

--- a/solution.py
+++ b/solution.py
@@ -174,7 +174,14 @@
         residual.astype(jnp.float32)
         + jnp.dot(values, out_weight, preferred_element_type=jnp.float32)
     ).astype(jnp.bfloat16)
-    gathered = lax.all_gather(hidden_out[None], ("seq", "mp"), axis=0, tiled=True)
+
+    def match_inputs_over_axis(sheet):
+        top = jnp.stack([sheet for _ in range(lax.axis_size(("seq", "mp")))], 0)
+        prior = lax.all_to_all(top, ("seq", "mp"), 0, 0)
+        taken_in = jnp.concatenate(prior, 0)
+        return taken_in
+
+    gathered = match_inputs_over_axis(hidden_out[None])
     all_rows = gathered.reshape(seq_count, mp_count, RQ, col_width).transpose(1, 2, 0, 3)
     all_rows = all_rows.reshape(mp_count * RQ, seq_count * col_width)
     rows_f = all_rows.astype(jnp.float32)

time: 445 us -> 404 us (0.908)
  blocking collectives: 297 us -> 228 us
  waiting for transfers between devices: 45.7 us -> 61.4 us
  starting transfers between devices: 17.2 us -> 26.5 us
    all_gather x1 -> x0, blocking collectives: 67.2 us -> none  [body(): lax.all_gather(hidden_out[None], ('seq', 'mp'), axis=0, tiled=True)]
    all_to_all x0 -> x1, waiting for transfers between devices: none -> 15.3 us  [match_inputs_over_axis(): prior = lax.all_to_all(top, ('seq', 'mp'), 0, 0)]
    all_to_all x0 -> x1, starting transfers between devices: none -> 9.24 us  [match_inputs_over_axis(): prior = lax.all_to_all(top, ('seq', 'mp'), 0, 0)]
  transfers between devices with their start and end apart: 3 -> 4, of which waited for: 2 -> 3; matrix products, arithmetic and copies ran while one was open for 2% -> 2% of each run, Pallas kernels for 0% -> 0%
where the time goes in v1:
time: 404 us; the launch traced here: 402 us
  blocking collectives  228 us (56%)
  waiting for transfers between devices  61.4 us (15%)
  local copies, waits for them, and re-layouts  46.8 us (12%)
  starting transfers between devices  26.5 us (7%)
  between operations  14.5 us (4%)
  other arithmetic  12.6 us (3%)
  matrix products  11.6 us (3%)
    all_gather x1, blocking collectives, body(): lax.all_gather(query_part, 'seq', axis=1, tiled=True)  88.3 us
    pmax x1, blocking collectives, body(): best_all = lax.pmax(local_best, ('seq', 'mp'))  72.6 us
    all_gather x2, blocking collectives, merged(): everything = jax.tree.map(lambda part: lax.all_gather(part, axis), x)  67.1 us
    all_gather x1, waiting for transfers between devices, merged(): everything = jax.tree.map(lambda part: lax.all_gather(part, axis), x)  41.9 us
    dynamic_slice x31, local copies, waits for them, and re-layouts, step(): return combine(so_far, jax.tree.map(lambda part: part[k], everything))  30.3 us
    all_to_all x1, waiting for transfers between devices, match_inputs_over_axis(): prior = lax.all_to_all(top, ('seq', 'mp'), 0, 0)  15.3 us
    all_to_all x1, starting transfers between devices, body(): lax.all_to_all(send_summary, 'seq', split_axis=0, concat_axis=0, tiled=True)  11.9 us
    all_to_all x1, starting transfers between devices, match_inputs_over_axis(): prior = lax.all_to_all(top, ('seq', 'mp'), 0, 0)  9.24 us
  transfers between devices with their start and end apart: 4, of which 3 were waited for; matrix products, arithmetic and copies ran while one was open for 2% of the time, Pallas kernels for 0%

profile of v1, /device:TPU:1, one launch (start us, length us, event | category | flops | bytes accessed | tf_op | source)
XLA Modules:
  0.0 402.2 jit_solution(15729309356285953773)
XLA Ops:
  7.2 1.0 dynamic-slice_reduce_fusion
  10.5 1.7 fusion.37
  14.5 11.9 %all-to-all-start.1 = ((bf16[32,2,288]{2,1,0:T(2,128)(2,1)}), bf16[32,2,288]{2,1,0:T(2,128)(2,1)S(1)}, u32[]{:S(2)}, u32[]{:S(2)}) async-start(bf16[32,2,288]{2,1,0:T(2,128)(2,1)} %reshape.206), calls=%async_computation.1 | async-start | bytes 98304 | tf_op jit(solution)/shard_map/all_to_all | solution.py:152
  26.3 1.2 convolution_convert_fusion
  28.6 2.4 copy.126
  31.0 4.1 %all-to-all-done.1 = bf16[32,2,288]{2,1,0:T(2,128)(2,1)S(1)} async-done(((bf16[32,2,288]{2,1,0:T(2,128)(2,1)}), bf16[32,2,288]{2,1,0:T(2,128)(2,1)S(1)}, u32[]{:S(2)}, u32[]{:S(2)}) %all-to-all-start.1) | async-done | bytes 36896 | tf_op jit(solution)/shard_map/all_to_all | solution.py:152
  35.1 5.3 %all-to-all-start = ((bf16[32,1,64,576]{3,2,1,0:T(8,128)(2,1)}), bf16[32,1,64,576]{3,2,1,0:T(8,128)(2,1)}, u32[]{:S(2)}, u32[]{:S(2)}) async-start(bf16[32,1,64,576]{3,2,1,0:T(8,128)(2,1)} %copy.126), calls=%async_computation | async-start | bytes 5242880 | tf_op jit(solution)/shard_map/all_to_all | solution.py:151
  40.8 88.3 %all-gather.3 = bf16[32,96,8]{1,2,0:T(8,128)(2,1)S(1)} all-gather(bf16[1,96,8]{1,2,0:T(8,128)(2,1)S(1)} %fusion.10), channel_id=1, replica_groups=mesh['seq'=32,'mp'=8] {'seq'}, dimensions={0}, use_global_device_ids=true | all-gather | bytes 50688 | tf_op jit(solution)/shard_map/all_gather | solution.py:117
  132.6 2.4 gather_fusion
  136.4 1.2 convolution_bitcast_fusion
  137.7 32.5 %all-gather = f32[256,16]{1,0:T(8,128)S(1)} all-gather(f32[8,16]{1,0:T(8,128)S(1)} %copy.132), channel_id=2, replica_groups=mesh['seq'=32,'mp'=8] {'seq'}, dimensions={0}, use_global_device_ids=true | all-gather | bytes 16896 | tf_op jit(solution)/shard_map/all_gather | solution.py:20
  170.5 34.6 %all-gather.1 = f32[256,16]{1,0:T(8,128)S(1)} all-gather(f32[8,16]{1,0:T(8,128)S(1)} %bitcast.114), channel_id=3, replica_groups=mesh['seq'=32,'mp'=8] {'seq'}, dimensions={0}, use_global_device_ids=true | all-gather | bytes 16896 | tf_op jit(solution)/shard_map/all_gather | solution.py:20
  205.0 41.9 %all-gather.6.cloned.1.call-done = f32[256,16,512]{2,0,1:T(8,128)} async-done(((f32[8,16,512]{2,0,1:T(8,128)}), f32[256,16,512]{2,0,1:T(8,128)}) %all-gather.6.cloned.1.call-update) | async-done | bytes 8388624 | tf_op jit(solution)/shard_map/all_gather | solution.py:20
  248.1 38.1 %while.19 = (s32[]{:T(128)}, f32[8,16]{1,0:T(8,128)S(1)}, f32[8,16]{1,0:T(8,128)S(1)}, f32[8,16,512]{2,1,0:T(8,128)S(1)}, f32[32,8,16]{2,1,0:T(8,128)S(1)}, /*in...) while((s32[]{:T(128)}, f32[8,16]{1,0:T(8,128)S(1)}, ...), condition=%wide.region_9.10_spmd, body=%wide.region_8.9_spmd.sunk | while | flops 197381 | bytes 1315991 | solution.py:26
  248.2 1.0 constant_dynamic-slice_fusion.2
  249.4 1.0 constant_dynamic-slice_fusion.2
  250.6 1.0 constant_dynamic-slice_fusion.2
  251.9 1.0 constant_dynamic-slice_fusion.2
  253.1 1.0 constant_dynamic-slice_fusion.2
  254.3 1.0 constant_dynamic-slice_fusion.2
  255.5 1.0 constant_dynamic-slice_fusion.2
  256.8 1.0 constant_dynamic-slice_fusion.2
  258.0 1.0 constant_dynamic-slice_fusion.2
  259.2 1.0 constant_dynamic-slice_fusion.2
  260.5 1.0 constant_dynamic-slice_fusion.2
  261.7 1.0 constant_dynamic-slice_fusion.2
  262.9 1.0 constant_dynamic-slice_fusion.2
  264.1 1.0 constant_dynamic-slice_fusion.2
  265.4 1.0 constant_dynamic-slice_fusion.2
  266.6 1.0 constant_dynamic-slice_fusion.2
  267.8 1.0 constant_dynamic-slice_fusion.2
  269.0 1.0 constant_dynamic-slice_fusion.2
  270.3 1.0 constant_dynamic-slice_fusion.2
  271.5 1.0 constant_dynamic-slice_fusion.2
  272.7 1.0 constant_dynamic-slice_fusion.2
  274.0 1.0 constant_dynamic-slice_fusion.2
  275.2 1.0 constant_dynamic-slice_fusion.2
  276.4 1.0 constant_dynamic-slice_fusion.2
  280.1 1.0 constant_dynamic-slice_fusion.2
  286.3 2.1 fusion.9
  288.6 1.0 reshape.208
  289.6 9.2 %all-to-all-start.2 = ((bf16[256,2,256]{2,1,0:T(2,128)(2,1)}), bf16[256,2,256]{2,1,0:T(2,128)(2,1)S(1)}, u32[]{:S(2)}, u32[]{:S(2)}) async-start(bf16[256,2,256]{2,1,0:T(2,128)(2,1)} %reshape.208), calls=%async_computation.2 | async-start | bytes 524288 | tf_op jit(solution)/shard_map/all_to_all | solution.py:180
  299.0 15.3 %all-to-all-done.2 = bf16[256,2,256]{2,1,0:T(2,128)(2,1)S(1)} async-done(((bf16[256,2,256]{2,1,0:T(2,128)(2,1)}), bf16[256,2,256]{2,1,0:T(2,128)(2,1)S(1)}, u32[]{:S(2)}, u32[]{:S(2)}) %all-to-all-start.2) | async-done | bytes 262176 | tf_op jit(solution)/shard_map/all_to_all | solution.py:180
  315.0 1.1 bitcast_convert_fusion
  316.2 1.8 copy.140
  318.1 1.1 reshape.151
  319.3 2.3 fusion.5
  321.6 72.6 %pmax.7 = f32[64]{0:T(128)S(1)} all-reduce(f32[64]{0:T(128)S(1)} %fusion.5), channel_id=1, replica_groups=mesh['seq'=32,'mp'=8] {'seq','mp'}, use_global_device_ids=true, to_apply=%region_15.16 | all-reduce | flops 64 | bytes 512 | tf_op jit(solution)/shard_map/pmax | solution.py:204
  (162 shorter events, 27.1 us)
Async XLA Ops:
  7.2 122.2 %copy-start = (bf16[16,128,512]{2,1,0:T(8,128)(2,1)S(1)}, bf16[16,128,512]{2,1,0:T(8,128)(2,1)}, u32[]{:S(2)}) copy-start(bf16[16,128,512]{2,1,0:T(8,128)(2,1)} %param.18) | copy-start | bytes 6291460
  7.2 19.2 %copy-start.1 = (bf16[8,128,576]{1,2,0:T(8,128)(2,1)S(1)}, bf16[8,128,576]{1,2,0:T(8,128)(2,1)}, u32[]{:S(2)}) copy-start(bf16[8,128,576]{1,2,0:T(8,128)(2,1)} %param.21) | copy-start | bytes 3538948
  14.5 20.7 %all-to-all-start.1 = ((bf16[32,2,288]{2,1,0:T(2,128)(2,1)}), bf16[32,2,288]{2,1,0:T(2,128)(2,1)S(1)}, u32[]{:S(2)}, u32[]{:S(2)}) async-start(bf16[32,2,288]{2,1,0:T(2,128)(2,1)} %reshape.206), calls=%async_computation.1 | async-start | bytes 98304 | tf_op jit(solution)/shard_map/all_to_all | solution.py:152
  31.0 9.6 %copy-start.3 = (bf16[2048,96]{0,1:T(8,128)(2,1)S(1)}, bf16[2048,96]{0,1:T(8,128)(2,1)}, u32[]{:S(2)}) copy-start(bf16[2048,96]{0,1:T(8,128)(2,1)} %param.17) | copy-start | bytes 1179652
  31.0 9.6 %copy-start.5 = (bf16[8,2048]{1,0:T(8,128)(2,1)S(1)}, bf16[8,2048]{1,0:T(8,128)(2,1)}, u32[]{:S(2)}) copy-start(bf16[8,2048]{1,0:T(8,128)(2,1)} %param.16) | copy-start | bytes 98308
  35.1 97.5 %all-to-all-start = ((bf16[32,1,64,576]{3,2,1,0:T(8,128)(2,1)}), bf16[32,1,64,576]{3,2,1,0:T(8,128)(2,1)}, u32[]{:S(2)}, u32[]{:S(2)}) async-start(bf16[32,1,64,576]{3,2,1,0:T(8,128)(2,1)} %copy.126), calls=%async_computation | async-start | bytes 5242880 | tf_op jit(solution)/shard_map/all_to_all | solution.py:151
  40.5 89.3 %copy-start.7 = (s32[8,32]{1,0:T(8,128)S(1)}, s32[8,32]{1,0:T(8,128)}, u32[]{:S(2)}) copy-start(s32[8,32]{1,0:T(8,128)} %param.25) | copy-start | bytes 3076
  40.5 206.4 %all-gather.6.cloned.1.call-start = ((), (), s32[]{:S(2)}) async-start(), calls=%async_computation.3 | async-start | bytes 8650752 | tf_op jit(solution)/shard_map/all_gather | solution.py:20
  132.2 115.9 %copy-start.6 = (bf16[4,576]{1,0:T(4,128)(2,1)}, bf16[4,576]{1,0:T(4,128)(2,1)S(1)}, u32[]{:S(2)}) copy-start(bf16[4,576]{1,0:T(4,128)(2,1)S(1)} %broadcast_select_fusion.7) | copy-start | bytes 13828
  135.1 113.0 %copy-start.2 = (bf16[4,64,576]{2,1,0:T(8,128)(2,1)}, bf16[4,64,576]{2,1,0:T(8,128)(2,1)S(1)}, u32[]{:S(2)}) copy-start(bf16[4,64,576]{2,1,0:T(8,128)(2,1)S(1)} %broadcast_select_fusion) | copy-start | bytes 884740
  248.1 38.2 %copy-start.4 = (bf16[2048,64]{0,1:T(8,128)(2,1)S(1)}, bf16[2048,64]{0,1:T(8,128)(2,1)}, u32[]{:S(2)}) copy-start(bf16[2048,64]{0,1:T(8,128)(2,1)} %param.20) | copy-start | bytes 786436
  286.3 12.6 %copy-start.9 = (bf16[2048]{0:T(1024)(128)(2,1)S(1)}, bf16[2048]{0:T(1024)(128)(2,1)}, u32[]{:S(2)}) copy-start(bf16[2048]{0:T(1024)(128)(2,1)} %param.26) | copy-start | bytes 12292
  286.3 12.6 %copy-start.10 = (s32[4,2]{0,1:T(2,128)S(1)}, s32[4,2]{0,1:T(2,128)}, u32[]{:S(2)}) copy-start(s32[4,2]{0,1:T(2,128)} %param.28) | copy-start | bytes 100
  286.3 12.6 %copy-start.11 = (s32[64]{0:T(128)S(1)}, s32[64]{0:T(128)}, u32[]{:S(2)}) copy-start(s32[64]{0:T(128)} %param.29) | copy-start | bytes 772
  288.5 27.6 %copy-start.8 = (bf16[8,64]{1,0:T(8,128)(2,1)}, bf16[8,64]{1,0:T(8,128)(2,1)S(1)}, u32[]{:S(2)}) copy-start(bf16[8,64]{1,0:T(8,128)(2,1)S(1)} %fusion.9) | copy-start | bytes 3076
  289.6 24.7 %all-to-all-start.2 = ((bf16[256,2,256]{2,1,0:T(2,128)(2,1)}), bf16[256,2,256]{2,1,0:T(2,128)(2,1)S(1)}, u32[]{:S(2)}, u32[]{:S(2)}) async-start(bf16[256,2,256]{2,1,0:T(2,128)(2,1)} %reshape.208), calls=%async_computation.2 | async-start | bytes 524288 | tf_op jit(solution)/shard_map/all_to_all | solution.py:180
Sparse Core Ops, SparseCore 0:
  137.7 109.1 all-gather.5
